TPU v7x, 32 devices: a whole 2x2x4 slice. The times are simulated.
32 devices in a mesh: member: 2 (over y), cell: 16 (over z, x, core).
Axes of the slice: x: 2, y: 2, z: 4, core: 2. Of those that a mesh axis runs over, the one named last changes fastest.
Arguments:
- wave_energy: float32 [2304, 2048], P(('member', 'cell')), parts along dimension 0, may hold values from -6 to 6
- courant: float32 [1152], replicated, may hold values from -0.9 to 0.9
- sea_mask: int32 [2048], replicated, may hold values 0 or 1
- lift_weight: bfloat16 [1024, 1152], replicated, may hold values from -0.1875 to 0.1875
- back_weight: bfloat16 [1152, 1024], replicated, may hold values from -0.1875 to 0.1875
Outputs:
- wave_next: float32 [2304, 2048], P(('member', 'cell')), parts along dimension 0
There are 2 independent parts, one for each index of `member`. A program takes and returns all parts, laid end to end along the dimension named above; an argument that names none is the same for every part. Nothing has to cross between parts.
All inputs are finite; a program needn't handle non-finite values.
Results may differ from a plain program's by a relative error of at most 0.0026.
Values sent between devices are 32-bit elements; how exact they have to be, the bound alone decides.
A program may use at most 64 MiB of HBM per device.

v0:
```python
import jax
import jax.numpy as jnp
from jax import lax
from jax.sharding import PartitionSpec as P

STEPS = 2


coupling = 0.25


def with_halo(value, sides, width):
    for axis, dim in sides:
        devices, length = (lax.axis_size(axis), value.shape[dim])
        up = [(i, (i + 1) % devices) for i in range(devices - 1)]
        down = [(j, i) for i, j in up]
        last = lax.slice_in_dim(value, length - width, length, axis=dim)
        first = lax.slice_in_dim(value, 0, width, axis=dim)
        before = lax.ppermute(last, axis, up)
        after = lax.ppermute(first, axis, down)
        value = jnp.concatenate([before, value, after], axis=dim)
    return value


def minmod(first_term, second_term):
    return (
        0.5
        * (jnp.sign(first_term) + jnp.sign(second_term))
        * jnp.minimum(jnp.abs(first_term), jnp.abs(second_term))
    )


def substep(spectra, sea_field, speeds):
    extent_cells = spectra.shape[1]
    differences = spectra[:, 1:] - spectra[:, :-1]
    slopes = minmod(differences[:, 1:], differences[:, :-1])
    forward_speed = jnp.maximum(speeds, 0.0)
    backward_speed = jnp.minimum(speeds, 0.0)
    open_faces = sea_field[1 : extent_cells - 2] * sea_field[2 : extent_cells - 1]
    fluxes = forward_speed * (
        spectra[:, 1 : extent_cells - 2]
        + 0.5 * (1.0 - forward_speed) * slopes[:, 0 : extent_cells - 3]
    )
    fluxes = fluxes + backward_speed * (
        spectra[:, 2 : extent_cells - 1]
        - 0.5 * (1.0 + backward_speed) * slopes[:, 1 : extent_cells - 2]
    )
    fluxes = fluxes * open_faces
    return spectra[:, 2 : extent_cells - 2] - (fluxes[:, 1:] - fluxes[:, :-1])


def shards(wave_energy, courant, sea_mask, lift_weight, back_weight):
    devices_count = lax.axis_size("cell")
    device_rank = lax.axis_index("cell")
    groups, all_cells = wave_energy.shape
    tile_cells = all_cells // devices_count
    sea_field = sea_mask.astype(jnp.float32)
    tile_state = lax.all_to_all(wave_energy, "cell", split_axis=1, concat_axis=0, tiled=True)
    speeds = courant[:, None]
    local_sea = lax.dynamic_slice_in_dim(
        jnp.pad(sea_field, 4), device_rank * tile_cells, tile_cells + 8
    )
    for repeat in range(STEPS):
        advance_tile_state = tile_state
        for turn_index in range(2):
            extended = with_halo(advance_tile_state, (("cell", 1),), 2)
            advance_tile_state = substep(extended, local_sea[2:-2], speeds)
        lifted = jnp.dot(
            lift_weight, advance_tile_state.astype(jnp.bfloat16), preferred_element_type=jnp.float32
        )
        squared = (lifted * lifted).astype(jnp.bfloat16)
        source = jnp.dot(back_weight, squared, preferred_element_type=jnp.float32)
        tile_state = advance_tile_state + coupling * source
    return lax.all_to_all(tile_state, "cell", split_axis=0, concat_axis=1, tiled=True)


def solution(mesh):
    placed = (P(("member", "cell"), None), P(), P(), P(), P())
    return jax.shard_map(
        shards, mesh=mesh, in_specs=placed, out_specs=P(("member", "cell"), None), check_vma=False
    )
```

profile of v0, /device:TPU:0, one launch (start us, length us, event | category | flops | bytes accessed | tf_op | source)
XLA Modules:
  0.0 93.8 jit_solution(6976342103805384461)
XLA Ops:
  0.0 2.1 %copy_bitcast_fusion.1 = f32[72,16,128]{2,0,1:T(8,128)} fusion(f32[72,2048]{1,0:T(8,128)} %param.5), kind=kLoop, calls=%fused_computation.63 | loop fusion | bytes 1179648 | tf_op jit(solution)/shard_map/all_to_all | solution.py:58
  2.1 7.4 %all-to-all-start = ((f32[72,16,128]{2,0,1:T(8,128)}), f32[72,16,128]{2,0,1:T(8,128)S(1)}, u32[]{:S(2)}, u32[]{:S(2)}) async-start(f32[72,16,128]{2,0,1:T(8,128)} %copy_bitcast_fusion.1), calls=%async_computation | async-start | bytes 1179648 | tf_op jit(solution)/shard_map/all_to_all | solution.py:58
  9.5 0.7 pad_dynamic-slice_fusion
  10.2 0.6 broadcast_maximum_fusion
  10.8 14.1 %all-to-all-done = f32[72,16,128]{2,0,1:T(8,128)S(1)} async-done(((f32[72,16,128]{2,0,1:T(8,128)}), f32[72,16,128]{2,0,1:T(8,128)S(1)}, u32[]{:S(2)}, u32[]{:S(2)}) %all-to-all-start) | async-done | bytes 589856 | tf_op jit(solution)/shard_map/all_to_all | solution.py:58
  24.8 0.2 copy.30
  25.1 2.1 %collective-permute-start = (f32[1152,2]{0,1:T(2,128)S(1)}, f32[1152,2]{0,1:T(2,128)S(1)}, u32[]{:S(2)}, u32[]{:S(2)}) collective-permute-start(f32[1152,2]{0,1:T(2,128)S(1)} %get-tuple-element.11), channel_id=1, source_target_pairs={{0,1},{1,2},{2,3},{3,4},{4,5},{5,6},{6,7},{7,8},{8,9},{9,10},{10,1... | collective-permute-start | bytes 27656 | tf_op jit(solution)/shard_map/ppermute | solution.py:19
  27.2 1.3 %collective-permute-start.1 = (f32[1152,2]{0,1:T(2,128)S(1)}, f32[1152,2]{0,1:T(2,128)S(1)}, u32[]{:S(2)}, u32[]{:S(2)}) collective-permute-start(f32[1152,2]{0,1:T(2,128)S(1)} %get-tuple-element.12), channel_id=1, source_target_pairs={{1,0},{2,1},{3,2},{4,3},{5,4},{6,5},{7,6},{8,7},{9,8},{10,9},{11,1... | collective-permute-start | bytes 27656 | tf_op jit(solution)/shard_map/ppermute | solution.py:20
  28.5 0.8 slice_multiply_fusion.8
  29.4 0.0 collective-permute-done
  29.4 0.9 collective-permute-done.1
  30.3 0.1 pad_maximum_fusion.8
  30.4 0.1 slice_subtract_fusion.3
  30.4 0.4 minimum_multiply_fusion.3
  30.9 0.0 copy-done.1
  30.9 0.3 fusion.27
  31.2 0.1 fusion.33
  31.3 4.3 %collective-permute-start.2 = (f32[1152,2]{0,1:T(2,128)S(1)}, f32[1152,2]{0,1:T(2,128)S(1)}, u32[]{:S(2)}, u32[]{:S(2)}) collective-permute-start(f32[1152,2]{0,1:T(2,128)S(1)} %get-tuple-element.9), channel_id=1, source_target_pairs={{0,1},{1,2},{2,3},{3,4},{4,5},{5,6},{6,7},{7,8},{8,9},{9,10},{10,1... | collective-permute-start | bytes 27656 | tf_op jit(solution)/shard_map/ppermute | solution.py:19
  35.6 1.3 %collective-permute-start.3 = (f32[1152,2]{0,1:T(2,128)S(1)}, f32[1152,2]{0,1:T(2,128)S(1)}, u32[]{:S(2)}, u32[]{:S(2)}) collective-permute-start(f32[1152,2]{0,1:T(2,128)S(1)} %get-tuple-element.10), channel_id=1, source_target_pairs={{1,0},{2,1},{3,2},{4,3},{5,4},{6,5},{7,6},{8,7},{9,8},{10,9},{11,1... | collective-permute-start | bytes 27656 | tf_op jit(solution)/shard_map/ppermute | solution.py:20
  36.9 0.0 collective-permute-done.2
  36.9 1.8 %collective-permute-done.3 = f32[1152,2]{0,1:T(2,128)S(1)} collective-permute-done((f32[1152,2]{0,1:T(2,128)S(1)}, f32[1152,2]{0,1:T(2,128)S(1)}, u32[]{:S(2)}, u32[]{:S(2)}) %collective-permute-start.3) | collective-permute-done | bytes 9248 | tf_op jit(solution)/shard_map/ppermute | solution.py:20
  38.7 0.1 pad_maximum_fusion.9
  38.8 0.1 slice_subtract_fusion.2
  38.8 0.4 minimum_multiply_fusion.2
  39.3 1.1 %fusion.21 = f32[1152,129]{0,1:T(8,128)} fusion(f32[1152,130]{0,1:T(8,128)S(1)} %minimum_multiply_fusion.2, f32[1152,2]{0,1:T(2,128)S(1)} %collective-permute-done.3, f32[1152,128]{0,1:T(8,128)S(1)} %fusion.33, f32[1152,2]{0,1:T(2,128)S(1)} %collective-permute-done.2, f32[129]{0:T(256)S(1)} %slice_multiply_fusion.8, f32[1152]{0:T(1024)S(1)} %get-tuple-element.14, ...), kind=kLoop, calls=%fused_computation.36 | loop fusion | flops 1486080 | bytes 2410500 | tf_op jit(solution)/shard_map/mul | solution.py:48
  40.4 4.2 %fusion.1 = f32[1152,128]{0,1:T(8,128)S(1)} fusion(bf16[1152,1024]{1,0:T(8,128)(2,1)S(1)} %copy-done, bf16[1024,1152]{1,0:T(8,128)(2,1)} %param.8, f32[1152,128]{0,1:T(8,128)S(1)} %fusion.33, f32[1152,129]{0,1:T(8,128)} %fusion.21), kind=kOutput, calls=%fused_computation.3 | convolution fusion | flops 605274112 | bytes 8847360 | tf_op jit(solution)/shard_map/dot_general | solution.py:72
  44.6 5.4 %collective-permute-start.4 = (f32[1152,2]{0,1:T(2,128)S(1)}, f32[1152,2]{0,1:T(2,128)S(1)}, u32[]{:S(2)}, u32[]{:S(2)}) collective-permute-start(f32[1152,2]{0,1:T(2,128)S(1)} %get-tuple-element.7), channel_id=1, source_target_pairs={{0,1},{1,2},{2,3},{3,4},{4,5},{5,6},{6,7},{7,8},{8,9},{9,10},{10,1... | collective-permute-start | bytes 27656 | tf_op jit(solution)/shard_map/ppermute | solution.py:19
  50.0 0.0 copy-start.6
  50.0 1.4 %collective-permute-start.5 = (f32[1152,2]{0,1:T(2,128)S(1)}, f32[1152,2]{0,1:T(2,128)S(1)}, u32[]{:S(2)}, u32[]{:S(2)}) collective-permute-start(f32[1152,2]{0,1:T(2,128)S(1)} %get-tuple-element.8), channel_id=1, source_target_pairs={{1,0},{2,1},{3,2},{4,3},{5,4},{6,5},{7,6},{8,7},{9,8},{10,9},{11,1... | collective-permute-start | bytes 27656 | tf_op jit(solution)/shard_map/ppermute | solution.py:20
  51.5 0.0 collective-permute-done.4
  51.5 1.8 %collective-permute-done.5 = f32[1152,2]{0,1:T(2,128)S(1)} collective-permute-done((f32[1152,2]{0,1:T(2,128)S(1)}, f32[1152,2]{0,1:T(2,128)S(1)}, u32[]{:S(2)}, u32[]{:S(2)}) %collective-permute-start.5) | collective-permute-done | bytes 9248 | tf_op jit(solution)/shard_map/ppermute | solution.py:20
  53.2 0.1 pad_maximum_fusion.10
  53.3 0.1 slice_subtract_fusion.1
  53.4 0.4 minimum_multiply_fusion.1
  53.8 0.3 fusion.15
  54.1 0.1 fusion.31
  54.2 4.7 %collective-permute-start.6 = (f32[1152,2]{0,1:T(2,128)S(1)}, f32[1152,2]{0,1:T(2,128)S(1)}, u32[]{:S(2)}, u32[]{:S(2)}) collective-permute-start(f32[1152,2]{0,1:T(2,128)S(1)} %get-tuple-element.5), channel_id=1, source_target_pairs={{0,1},{1,2},{2,3},{3,4},{4,5},{5,6},{6,7},{7,8},{8,9},{9,10},{10,1... | collective-permute-start | bytes 27656 | tf_op jit(solution)/shard_map/ppermute | solution.py:19
  59.0 1.3 %collective-permute-start.7 = (f32[1152,2]{0,1:T(2,128)S(1)}, f32[1152,2]{0,1:T(2,128)S(1)}, u32[]{:S(2)}, u32[]{:S(2)}) collective-permute-start(f32[1152,2]{0,1:T(2,128)S(1)} %get-tuple-element.6), channel_id=1, source_target_pairs={{1,0},{2,1},{3,2},{4,3},{5,4},{6,5},{7,6},{8,7},{9,8},{10,9},{11,1... | collective-permute-start | bytes 27656 | tf_op jit(solution)/shard_map/ppermute | solution.py:20
  60.3 0.0 collective-permute-done.6
  60.3 1.8 %collective-permute-done.7 = f32[1152,2]{0,1:T(2,128)S(1)} collective-permute-done((f32[1152,2]{0,1:T(2,128)S(1)}, f32[1152,2]{0,1:T(2,128)S(1)}, u32[]{:S(2)}, u32[]{:S(2)}) %collective-permute-start.7) | collective-permute-done | bytes 9248 | tf_op jit(solution)/shard_map/ppermute | solution.py:20
  62.0 0.1 pad_maximum_fusion.11
  62.1 0.1 slice_subtract_fusion
  62.2 0.4 minimum_multiply_fusion
  62.6 1.1 %fusion.9 = f32[1152,129]{0,1:T(8,128)} fusion(f32[1152,130]{0,1:T(8,128)S(1)} %minimum_multiply_fusion, f32[1152,2]{0,1:T(2,128)S(1)} %collective-permute-done.7, f32[1152,128]{0,1:T(8,128)S(1)} %fusion.31, f32[1152,2]{0,1:T(2,128)S(1)} %collective-permute-done.6, f32[129]{0:T(256)S(1)} %copy-done.6, f32[1152]{0:T(1024)S(1)} %get-tuple-element.14, ...), kind=kLoop, calls=%fused_computation.14 | loop fusion | flops 1486080 | bytes 2410500 | tf_op jit(solution)/shard_map/mul | solution.py:48
  63.8 4.2 %fusion.3 = f32[1152,128]{0,1:T(8,128)S(1)} fusion(bf16[1152,1024]{1,0:T(8,128)(2,1)S(1)} %copy-done, bf16[1024,1152]{1,0:T(8,128)(2,1)} %param.8, f32[1152,128]{0,1:T(8,128)S(1)} %fusion.31, f32[1152,129]{0,1:T(8,128)} %fusion.9), kind=kOutput, calls=%fused_computation.5 | convolution fusion | flops 605274112 | bytes 8847360 | tf_op jit(solution)/shard_map/dot_general | solution.py:72
  67.9 0.2 copy.31
  68.2 24.7 %all_to_all.38 = f32[16,72,128]{2,1,0:T(8,128)S(1)} all-to-all(f32[16,72,128]{2,1,0:T(8,128)S(1)} %bitcast.28), channel_id=1, replica_groups=mesh['member'=2,'cell'=16] {'cell'}, dimensions={0} | all-to-all | bytes 1179648 | tf_op jit(solution)/shard_map/all_to_all | solution.py:74
  92.9 0.9 copy_bitcast_fusion
  (21 shorter events, 0.1 us)
Async XLA Ops:
  0.0 40.4 %copy-start = (bf16[1152,1024]{1,0:T(8,128)(2,1)S(1)}, bf16[1152,1024]{1,0:T(8,128)(2,1)}, u32[]{:S(2)}) copy-start(bf16[1152,1024]{1,0:T(8,128)(2,1)} %param.9) | copy-start | bytes 7077892
  0.0 9.5 %copy-start.8 = (s32[2048]{0:T(1024)S(1)}, s32[2048]{0:T(1024)}, u32[]{:S(2)}) copy-start(s32[2048]{0:T(1024)} %param.7) | copy-start | bytes 24580
  0.0 10.2 %copy-start.7 = (f32[1152]{0:T(1024)S(1)}, f32[1152]{0:T(1024)}, u32[]{:S(2)}) copy-start(f32[1152]{0:T(1024)} %param.6) | copy-start | bytes 13828
  2.1 22.8 %all-to-all-start = ((f32[72,16,128]{2,0,1:T(8,128)}), f32[72,16,128]{2,0,1:T(8,128)S(1)}, u32[]{:S(2)}, u32[]{:S(2)}) async-start(f32[72,16,128]{2,0,1:T(8,128)} %copy_bitcast_fusion.1), calls=%async_computation | async-start | bytes 1179648 | tf_op jit(solution)/shard_map/all_to_all | solution.py:58
  25.1 4.3 %collective-permute-start = (f32[1152,2]{0,1:T(2,128)S(1)}, f32[1152,2]{0,1:T(2,128)S(1)}, u32[]{:S(2)}, u32[]{:S(2)}) collective-permute-start(f32[1152,2]{0,1:T(2,128)S(1)} %get-tuple-element.11), channel_id=1, source_target_pairs={{0,1},{1,2},{2,3},{3,4},{4,5},{5,6},{6,7},{7,8},{8,9},{9,10},{10,1... | collective-permute-start | bytes 27656 | tf_op jit(solution)/shard_map/ppermute | solution.py:19
  27.2 3.1 %collective-permute-start.1 = (f32[1152,2]{0,1:T(2,128)S(1)}, f32[1152,2]{0,1:T(2,128)S(1)}, u32[]{:S(2)}, u32[]{:S(2)}) collective-permute-start(f32[1152,2]{0,1:T(2,128)S(1)} %get-tuple-element.12), channel_id=1, source_target_pairs={{1,0},{2,1},{3,2},{4,3},{5,4},{6,5},{7,6},{8,7},{9,8},{10,9},{11,1... | collective-permute-start | bytes 27656 | tf_op jit(solution)/shard_map/ppermute | solution.py:20
  29.4 9.9 %copy-start.5 = (f32[129]{0:T(256)}, f32[129]{0:T(256)S(1)}, u32[]{:S(2)}) copy-start(f32[129]{0:T(256)S(1)} %slice_multiply_fusion.8) | copy-start | bytes 1552
  29.4 1.5 %copy-start.1 = (f32[1152]{0:T(1024)S(1)}, f32[1152]{0:T(1024)}, u32[]{:S(2)}) copy-start(f32[1152]{0:T(1024)} %get-tuple-element.15) | copy-start | bytes 13828
  29.4 1.5 %copy-start.3 = (f32[1152]{0:T(1024)S(1)}, f32[1152]{0:T(1024)}, u32[]{:S(2)}) copy-start(f32[1152]{0:T(1024)} %get-tuple-element.16) | copy-start | bytes 13828
  31.3 5.6 %collective-permute-start.2 = (f32[1152,2]{0,1:T(2,128)S(1)}, f32[1152,2]{0,1:T(2,128)S(1)}, u32[]{:S(2)}, u32[]{:S(2)}) collective-permute-start(f32[1152,2]{0,1:T(2,128)S(1)} %get-tuple-element.9), channel_id=1, source_target_pairs={{0,1},{1,2},{2,3},{3,4},{4,5},{5,6},{6,7},{7,8},{8,9},{9,10},{10,1... | collective-permute-start | bytes 27656 | tf_op jit(solution)/shard_map/ppermute | solution.py:19
  35.6 3.1 %collective-permute-start.3 = (f32[1152,2]{0,1:T(2,128)S(1)}, f32[1152,2]{0,1:T(2,128)S(1)}, u32[]{:S(2)}, u32[]{:S(2)}) collective-permute-start(f32[1152,2]{0,1:T(2,128)S(1)} %get-tuple-element.10), channel_id=1, source_target_pairs={{1,0},{2,1},{3,2},{4,3},{5,4},{6,5},{7,6},{8,7},{9,8},{10,9},{11,1... | collective-permute-start | bytes 27656 | tf_op jit(solution)/shard_map/ppermute | solution.py:20
  44.6 6.8 %collective-permute-start.4 = (f32[1152,2]{0,1:T(2,128)S(1)}, f32[1152,2]{0,1:T(2,128)S(1)}, u32[]{:S(2)}, u32[]{:S(2)}) collective-permute-start(f32[1152,2]{0,1:T(2,128)S(1)} %get-tuple-element.7), channel_id=1, source_target_pairs={{0,1},{1,2},{2,3},{3,4},{4,5},{5,6},{6,7},{7,8},{8,9},{9,10},{10,1... | collective-permute-start | bytes 27656 | tf_op jit(solution)/shard_map/ppermute | solution.py:19
  50.0 3.8 %copy-start.2 = (f32[1152]{0:T(1024)S(1)}, f32[1152]{0:T(1024)}, u32[]{:S(2)}) copy-start(f32[1152]{0:T(1024)} %get-tuple-element.15) | copy-start | bytes 13828
  50.0 3.8 %copy-start.4 = (f32[1152]{0:T(1024)S(1)}, f32[1152]{0:T(1024)}, u32[]{:S(2)}) copy-start(f32[1152]{0:T(1024)} %get-tuple-element.16) | copy-start | bytes 13828
  50.0 3.8 %copy-start.6 = (f32[129]{0:T(256)S(1)}, f32[129]{0:T(256)}, u32[]{:S(2)}) copy-start(f32[129]{0:T(256)} %copy-done.5) | copy-start | bytes 1552
  50.0 3.2 %collective-permute-start.5 = (f32[1152,2]{0,1:T(2,128)S(1)}, f32[1152,2]{0,1:T(2,128)S(1)}, u32[]{:S(2)}, u32[]{:S(2)}) collective-permute-start(f32[1152,2]{0,1:T(2,128)S(1)} %get-tuple-element.8), channel_id=1, source_target_pairs={{1,0},{2,1},{3,2},{4,3},{5,4},{6,5},{7,6},{8,7},{9,8},{10,9},{11,1... | collective-permute-start | bytes 27656 | tf_op jit(solution)/shard_map/ppermute | solution.py:20
  54.2 6.1 %collective-permute-start.6 = (f32[1152,2]{0,1:T(2,128)S(1)}, f32[1152,2]{0,1:T(2,128)S(1)}, u32[]{:S(2)}, u32[]{:S(2)}) collective-permute-start(f32[1152,2]{0,1:T(2,128)S(1)} %get-tuple-element.5), channel_id=1, source_target_pairs={{0,1},{1,2},{2,3},{3,4},{4,5},{5,6},{6,7},{7,8},{8,9},{9,10},{10,1... | collective-permute-start | bytes 27656 | tf_op jit(solution)/shard_map/ppermute | solution.py:19
  59.0 3.1 %collective-permute-start.7 = (f32[1152,2]{0,1:T(2,128)S(1)}, f32[1152,2]{0,1:T(2,128)S(1)}, u32[]{:S(2)}, u32[]{:S(2)}) collective-permute-start(f32[1152,2]{0,1:T(2,128)S(1)} %get-tuple-element.6), channel_id=1, source_target_pairs={{1,0},{2,1},{3,2},{4,3},{5,4},{6,5},{7,6},{8,7},{9,8},{10,9},{11,1... | collective-permute-start | bytes 27656 | tf_op jit(solution)/shard_map/ppermute | solution.py:20
where the time goes:
time: 94.3 us; the launch traced here: 93.8 us
  starting transfers between devices  29.2 us (31%)
  blocking collectives  24.7 us (26%)
  waiting for transfers between devices  20.3 us (22%)
  matrix products  8.34 us (9%)
  other arithmetic  6.69 us (7%)
  local copies, waits for them, and re-layouts  4.13 us (4%)
    all_to_all x1, blocking collectives, shards(): lax.all_to_all(tile_state, 'cell', split_axis=0, concat_axis=1, tiled=True)  24.7 us
    ppermute x4, starting transfers between devices, with_halo(): before = lax.ppermute(last, axis, up)  16.6 us
    all_to_all x1, waiting for transfers between devices, shards(): lax.all_to_all(wave_energy, 'cell', split_axis=1, concat_axis=0, tiled=True)  14.1 us
    dot_general x2, matrix products, shards(): source = jnp.dot(back_weight, squared, preferred_element_type=jnp.float32)  8.34 us
    all_to_all x1, starting transfers between devices, shards(): lax.all_to_all(wave_energy, 'cell', split_axis=1, concat_axis=0, tiled=True)  7.39 us
    ppermute x4, waiting for transfers between devices, with_halo(): after = lax.ppermute(first, axis, down)  6.2 us
    ppermute x4, starting transfers between devices, with_halo(): after = lax.ppermute(first, axis, down)  5.3 us
    mul x4, other arithmetic, substep(): fluxes = fluxes * open_faces  2.82 us
  transfers between devices with their start and end apart: 9, of which 5 were waited for; matrix products, arithmetic and copies ran while one was open for 2% of the time, Pallas kernels for 0%

commit v1 on v0

--- a/solution.py
+++ b/solution.py
@@ -49,28 +49,33 @@
     return spectra[:, 2 : extent_cells - 2] - (fluxes[:, 1:] - fluxes[:, :-1])
 
 
+def fourwave(state, lift_weight, back_weight):
+    lifted = jnp.dot(lift_weight, state.astype(jnp.bfloat16), preferred_element_type=jnp.float32)
+    squared = (lifted * lifted).astype(jnp.bfloat16)
+    source = jnp.dot(back_weight, squared, preferred_element_type=jnp.float32)
+    return state + coupling * source
+
+
 def shards(wave_energy, courant, sea_mask, lift_weight, back_weight):
     devices_count = lax.axis_size("cell")
     device_rank = lax.axis_index("cell")
     groups, all_cells = wave_energy.shape
     tile_cells = all_cells // devices_count
     sea_field = sea_mask.astype(jnp.float32)
-    tile_state = lax.all_to_all(wave_energy, "cell", split_axis=1, concat_axis=0, tiled=True)
+    first_speeds = lax.dynamic_slice_in_dim(courant, device_rank * groups, groups)[:, None]
+    local = jnp.pad(wave_energy, ((0, 0), (4, 4)))
+    padded_sea = jnp.pad(sea_field, 4)
+    local = substep(local, padded_sea, first_speeds)
+    local = substep(local, padded_sea[2:-2], first_speeds)
+    tile_state = lax.all_to_all(local, "cell", split_axis=1, concat_axis=0, tiled=True)
     speeds = courant[:, None]
-    local_sea = lax.dynamic_slice_in_dim(
-        jnp.pad(sea_field, 4), device_rank * tile_cells, tile_cells + 8
-    )
-    for repeat in range(STEPS):
-        advance_tile_state = tile_state
-        for turn_index in range(2):
-            extended = with_halo(advance_tile_state, (("cell", 1),), 2)
-            advance_tile_state = substep(extended, local_sea[2:-2], speeds)
-        lifted = jnp.dot(
-            lift_weight, advance_tile_state.astype(jnp.bfloat16), preferred_element_type=jnp.float32
-        )
-        squared = (lifted * lifted).astype(jnp.bfloat16)
-        source = jnp.dot(back_weight, squared, preferred_element_type=jnp.float32)
-        tile_state = advance_tile_state + coupling * source
+    local_sea = lax.dynamic_slice_in_dim(padded_sea, device_rank * tile_cells, tile_cells + 8)
+    tile_state = fourwave(tile_state, lift_weight, back_weight)
+    for repeat in range(STEPS - 1):
+        extended = with_halo(tile_state, (("cell", 1),), 4)
+        extended = substep(extended, local_sea, speeds)
+        tile_state = substep(extended, local_sea[2:-2], speeds)
+        tile_state = fourwave(tile_state, lift_weight, back_weight)
     return lax.all_to_all(tile_state, "cell", split_axis=0, concat_axis=1, tiled=True)
 
 

time: 94.3 us -> 75.8 us (0.80)
  starting transfers between devices: 29.2 us -> 10.8 us
  other arithmetic: 6.69 us -> 12.9 us
  waiting for transfers between devices: 20.3 us -> 15 us
    ppermute x4 -> x1, starting transfers between devices: 16.6 us -> 2.14 us  [with_halo(): before = lax.ppermute(last, axis, up)]
    ppermute x4 -> x1, waiting for transfers between devices: 6.2 us -> 0.95 us  [with_halo(): after = lax.ppermute(first, axis, down)]
    ppermute x4 -> x1, starting transfers between devices: 5.3 us -> 1.29 us  [with_halo(): after = lax.ppermute(first, axis, down)]
    sub x4, other arithmetic: 0.26 us -> 2.15 us  [substep(): differences = spectra[:, 1:] - spectra[:, :-1]]
    all_to_all x2 -> x1, local copies, waits for them, and re-layouts: 2.29 us -> 1.05 us  [shards(): lax.all_to_all(local, 'cell', split_axis=1, concat_axis=0, tiled=True)]
    mul x4, other arithmetic: 2.82 us -> 4.05 us  [substep(): fluxes = fluxes * open_faces]
    all_to_all x0 -> x1, other arithmetic: none -> 1.19 us  [shards(): lax.all_to_all(local, 'cell', split_axis=1, concat_axis=0, tiled=True)]
    add x1, local copies, waits for them, and re-layouts: 0.23 us -> 1.29 us  [fourwave(): return state + coupling * source]
  transfers between devices with their start and end apart: 9 -> 3, of which waited for: 5 -> 2; matrix products, arithmetic and copies ran while one was open for 2% -> 3% of each run, Pallas kernels for 0% -> 0%
where the time goes in v1:
time: 75.8 us; the launch traced here: 75.3 us
  blocking collectives  25 us (33%)
  waiting for transfers between devices  15 us (20%)
  other arithmetic  12.9 us (17%)
  starting transfers between devices  10.8 us (14%)
  matrix products  8.12 us (11%)
  local copies, waits for them, and re-layouts  3.32 us (4%)
    all_to_all x1, blocking collectives, shards(): lax.all_to_all(tile_state, 'cell', split_axis=0, concat_axis=1, tiled=True)  25 us
    all_to_all x1, waiting for transfers between devices, shards(): lax.all_to_all(local, 'cell', split_axis=1, concat_axis=0, tiled=True)  14 us
    dot_general x2, matrix products, fourwave(): source = jnp.dot(back_weight, squared, preferred_element_type=jnp.float32)  8.12 us
    all_to_all x1, starting transfers between devices, shards(): lax.all_to_all(local, 'cell', split_axis=1, concat_axis=0, tiled=True)  7.39 us
    mul x4, other arithmetic, substep(): fluxes = fluxes * open_faces  4.05 us
    sub x4, other arithmetic, substep(): differences = spectra[:, 1:] - spectra[:, :-1]  2.15 us
    ppermute x1, starting transfers between devices, with_halo(): before = lax.ppermute(last, axis, up)  2.14 us
    mul x4, other arithmetic, minmod(): 0.5 * (jnp.sign(first_term) + jnp.sign(second_term))  1.79 us
  transfers between devices with their start and end apart: 3, of which 2 were waited for; matrix products, arithmetic and copies ran while one was open for 3% of the time, Pallas kernels for 0%

profile of v1, /device:TPU:0, one launch (start us, length us, event | category | flops | bytes accessed | tf_op | source)
XLA Modules:
  0.0 75.3 jit_solution(2506818184725759410)
XLA Ops:
  0.0 0.0 copy-start
  0.0 0.0 copy-start.5
  0.0 0.9 %convert_element_type.21 = f32[2048]{0:T(1024)S(1)} convert(s32[2048]{0:T(1024)} %param.7) | non-fusion elementwise | flops 2048 | bytes 16384 | tf_op jit(solution)/shard_map/convert_element_type | solution.py:64
  0.9 0.1 fusion.41
  0.9 0.1 fusion.42
  1.0 1.8 %slice_subtract_fusion.5 = f32[72,2055]{1,0:T(8,128)S(1)} fusion(f32[72,2048]{1,0:T(8,128)} %param.5), kind=kLoop, calls=%fused_computation.54 | loop fusion | flops 147960 | bytes 1181664 | tf_op jit(solution)/shard_map/sub | solution.py:35
  2.8 0.4 minimum_multiply_fusion.3
  3.3 0.0 copy-done.5
  3.3 0.0 copy-start.1
  3.3 0.1 subtract_multiply_fusion.1
  3.4 2.0 %fusion.29 = f32[72,2053]{1,0:T(8,128)S(1)} fusion(f32[72,2054]{1,0:T(8,128)S(1)} %minimum_multiply_fusion.3, f32[72,2048]{1,0:T(8,128)} %param.5, f32[2053]{0:T(1024)S(1)} %fusion.41, f32[72]{0:T(128)S(1)} %get-tuple-element.15, f32[72]{0:T(128)S(1)} %get-tuple-element.16, f32[72]{0:T(128)S(1)} %get-tuple-element.5, f32[72]{0:T(128)S(1)} %get-tuple-element.6), kind=kLoop, calls=%fused_computation.45 | loop fusion | flops 1182528 | bytes 2372980 | tf_op jit(solution)/shard_map/mul | solution.py:48
  5.4 0.0 copy-done.1
  5.4 0.4 fusion.25
  5.8 0.2 slice_subtract_fusion.3
  6.0 0.4 minimum_multiply_fusion.2
  6.5 0.6 fusion.22
  7.1 1.2 %copy_bitcast_fusion.1 = f32[72,16,128]{2,0,1:T(8,128)} fusion(f32[72,2049]{1,0:T(8,128)S(1)} %fusion.22, f32[72,2052]{1,0:T(8,128)S(1)} %fusion.25), kind=kLoop, calls=%fused_computation.56 | loop fusion | flops 294912 | bytes 2359296 | tf_op jit(solution)/shard_map/all_to_all | solution.py:70
  8.3 7.4 %all-to-all-start = ((f32[72,16,128]{2,0,1:T(8,128)}), f32[72,16,128]{2,0,1:T(8,128)S(1)}, u32[]{:S(2)}, u32[]{:S(2)}) async-start(f32[72,16,128]{2,0,1:T(8,128)} %copy_bitcast_fusion.1), calls=%async_computation | async-start | bytes 1179648 | tf_op jit(solution)/shard_map/all_to_all | solution.py:70
  15.7 0.1 pad_dynamic-slice_fusion
  15.8 0.6 slice_multiply_fusion.9
  16.4 0.6 broadcast_maximum_fusion
  17.0 14.0 %all-to-all-done = f32[72,16,128]{2,0,1:T(8,128)S(1)} async-done(((f32[72,16,128]{2,0,1:T(8,128)}), f32[72,16,128]{2,0,1:T(8,128)S(1)}, u32[]{:S(2)}, u32[]{:S(2)}) %all-to-all-start) | async-done | bytes 589856 | tf_op jit(solution)/shard_map/all_to_all | solution.py:70
  31.1 0.0 copy-done.4
  31.1 1.1 %copy.15 = f32[1152,128]{0,1:T(8,128)} copy(f32[1152,128]{1,0:T(8,128)S(1)} %bitcast.27) | data formatting | bytes 1179648 | tf_op jit(solution)/shard_map/all_to_all | solution.py:70
  32.1 0.0 copy-done
  32.1 3.3 %fusion.1 = f32[1152,128]{0,1:T(8,128)S(1)} fusion(f32[1152,128]{0,1:T(8,128)} %copy.15, bf16[1152,1024]{1,0:T(8,128)(2,1)S(1)} %copy-done, bf16[1024,1152]{1,0:T(8,128)(2,1)} %param.8, f32[1152,128]{1,0:T(8,128)S(1)} %bitcast.28), kind=kOutput, calls=%fused_computation.3 | convolution fusion | flops 604684288 | bytes 6488064 | tf_op jit(solution)/shard_map/dot_general | solution.py:55
  35.5 2.1 %collective-permute-start = (f32[1152,4]{0,1:T(4,128)S(1)}, f32[1152,4]{0,1:T(4,128)S(1)}, u32[]{:S(2)}, u32[]{:S(2)}) collective-permute-start(f32[1152,4]{0,1:T(4,128)S(1)} %get-tuple-element.9), channel_id=1, source_target_pairs={{0,1},{1,2},{2,3},{3,4},{4,5},{5,6},{6,7},{7,8},{8,9},{9,10},{10,1... | collective-permute-start | bytes 55304 | tf_op jit(solution)/shard_map/ppermute | solution.py:19
  37.6 1.3 %collective-permute-start.1 = (f32[1152,4]{0,1:T(4,128)S(1)}, f32[1152,4]{0,1:T(4,128)S(1)}, u32[]{:S(2)}, u32[]{:S(2)}) collective-permute-start(f32[1152,4]{0,1:T(4,128)S(1)} %get-tuple-element.10), channel_id=1, source_target_pairs={{1,0},{2,1},{3,2},{4,3},{5,4},{6,5},{7,6},{8,7},{9,8},{10,9},{11,1... | collective-permute-start | bytes 55304 | tf_op jit(solution)/shard_map/ppermute | solution.py:20
  38.9 0.8 %slice_multiply_fusion.8 = f32[129]{0:T(256)S(1)} fusion(f32[136]{0:T(256)} %copy-done.4), kind=kLoop, calls=%fused_computation.75 | loop fusion | flops 129 | bytes 1548 | tf_op jit(solution)/shard_map/mul | solution.py:39
  39.7 0.0 copy-start.2
  39.7 0.0 copy-start.3
  39.7 0.0 collective-permute-done
  39.8 0.9 %collective-permute-done.1 = f32[1152,4]{0,1:T(4,128)S(1)} collective-permute-done((f32[1152,4]{0,1:T(4,128)S(1)}, f32[1152,4]{0,1:T(4,128)S(1)}, u32[]{:S(2)}, u32[]{:S(2)}) %collective-permute-start.1) | collective-permute-done | bytes 18464 | tf_op jit(solution)/shard_map/ppermute | solution.py:20
  40.7 0.1 pad_maximum_fusion
  40.8 0.1 slice_subtract_fusion.2
  40.8 0.4 minimum_multiply_fusion.1
  41.3 0.0 copy-done.2
  41.3 0.0 copy-done.3
  41.3 0.0 copy-done.6
  41.3 0.3 fusion.16
  41.6 0.1 fusion.12
  41.8 0.1 slice_subtract_fusion
  41.8 0.4 minimum_multiply_fusion
  42.3 1.1 %fusion.9 = f32[1152,129]{0,1:T(8,128)} fusion(f32[1152,130]{0,1:T(8,128)S(1)} %minimum_multiply_fusion, f32[1152,132]{0,1:T(8,128)S(1)} %fusion.12, f32[129]{0:T(256)S(1)} %slice_multiply_fusion.8, f32[1152]{0:T(1024)S(1)} %get-tuple-element.12, f32[1152]{0:T(1024)S(1)} %copy-done.3, f32[1152]{0:T(1024)S(1)} %copy-done.2, f32[1152]{0:T(1024)S(1)} %get-tuple-element.11), kind=kLoop, calls=%fused_computation.14 | loop fusion | flops 1188864 | bytes 2991108 | tf_op jit(solution)/shard_map/mul | solution.py:48
  43.4 4.8 %fusion.3 = f32[1152,128]{0,1:T(8,128)} fusion(bf16[1152,1024]{1,0:T(8,128)(2,1)S(1)} %copy-done, bf16[1024,1152]{1,0:T(8,128)(2,1)} %param.8, f32[1152,129]{0,1:T(8,128)} %fusion.9, f32[1152,132]{0,1:T(8,128)S(1)} %fusion.12), kind=kOutput, calls=%fused_computation.5 | convolution fusion | flops 605274112 | bytes 8847360 | tf_op jit(solution)/shard_map/dot_general | solution.py:55
  48.2 1.3 %copy.16 = f32[1152,128]{1,0:T(8,128)S(1)} copy(f32[1152,128]{0,1:T(8,128)} %fusion.3) | data formatting | bytes 1179648 | tf_op jit(solution)/shard_map/add | solution.py:56
  49.5 25.0 %all_to_all.38 = f32[16,72,128]{2,1,0:T(8,128)S(1)} all-to-all(f32[16,72,128]{2,1,0:T(8,128)S(1)} %bitcast.29), channel_id=1, replica_groups=mesh['member'=2,'cell'=16] {'cell'}, dimensions={0} | all-to-all | bytes 1179648 | tf_op jit(solution)/shard_map/all_to_all | solution.py:79
  74.5 0.9 %copy_bitcast_fusion = f32[72,2048]{1,0:T(8,128)} fusion(f32[16,72,128]{2,1,0:T(8,128)S(1)} %all_to_all.38), kind=kLoop, calls=%fused_computation.55 | loop fusion | bytes 1179648 | tf_op jit(solution)/shard_map/all_to_all | solution.py:79
  (3 shorter events, 0.0 us)
Async XLA Ops:
  0.0 32.1 %copy-start = (bf16[1152,1024]{1,0:T(8,128)(2,1)S(1)}, bf16[1152,1024]{1,0:T(8,128)(2,1)}, u32[]{:S(2)}) copy-start(bf16[1152,1024]{1,0:T(8,128)(2,1)} %param.9) | copy-start | bytes 7077892
  0.0 3.3 %copy-start.5 = (f32[1152]{0:T(1024)S(1)}, f32[1152]{0:T(1024)}, u32[]{:S(2)}) copy-start(f32[1152]{0:T(1024)} %param.6) | copy-start | bytes 13828
  3.3 2.1 %copy-start.1 = (f32[72,2048]{1,0:T(8,128)S(1)}, f32[72,2048]{1,0:T(8,128)}, u32[]{:S(2)}) copy-start(f32[72,2048]{1,0:T(8,128)} %param.5) | copy-start | bytes 1769476
  8.3 22.8 %all-to-all-start = ((f32[72,16,128]{2,0,1:T(8,128)}), f32[72,16,128]{2,0,1:T(8,128)S(1)}, u32[]{:S(2)}, u32[]{:S(2)}) async-start(f32[72,16,128]{2,0,1:T(8,128)} %copy_bitcast_fusion.1), calls=%async_computation | async-start | bytes 1179648 | tf_op jit(solution)/shard_map/all_to_all | solution.py:70
  15.8 15.3 %copy-start.4 = (f32[136]{0:T(256)}, f32[136]{0:T(256)S(1)}, u32[]{:S(2)}) copy-start(f32[136]{0:T(256)S(1)} %pad_dynamic-slice_fusion) | copy-start | bytes 1636
  35.5 4.3 %collective-permute-start = (f32[1152,4]{0,1:T(4,128)S(1)}, f32[1152,4]{0,1:T(4,128)S(1)}, u32[]{:S(2)}, u32[]{:S(2)}) collective-permute-start(f32[1152,4]{0,1:T(4,128)S(1)} %get-tuple-element.9), channel_id=1, source_target_pairs={{0,1},{1,2},{2,3},{3,4},{4,5},{5,6},{6,7},{7,8},{8,9},{9,10},{10,1... | collective-permute-start | bytes 55304 | tf_op jit(solution)/shard_map/ppermute | solution.py:19
  37.6 3.1 %collective-permute-start.1 = (f32[1152,4]{0,1:T(4,128)S(1)}, f32[1152,4]{0,1:T(4,128)S(1)}, u32[]{:S(2)}, u32[]{:S(2)}) collective-permute-start(f32[1152,4]{0,1:T(4,128)S(1)} %get-tuple-element.10), channel_id=1, source_target_pairs={{1,0},{2,1},{3,2},{4,3},{5,4},{6,5},{7,6},{8,7},{9,8},{10,9},{11,1... | collective-permute-start | bytes 55304 | tf_op jit(solution)/shard_map/ppermute | solution.py:20
  39.7 1.6 %copy-start.2 = (f32[1152]{0:T(1024)S(1)}, f32[1152]{0:T(1024)}, u32[]{:S(2)}) copy-start(f32[1152]{0:T(1024)} %get-tuple-element.13) | copy-start | bytes 13828
  39.7 1.6 %copy-start.3 = (f32[1152]{0:T(1024)S(1)}, f32[1152]{0:T(1024)}, u32[]{:S(2)}) copy-start(f32[1152]{0:T(1024)} %get-tuple-element.14) | copy-start | bytes 13828
  39.7 1.6 %copy-start.6 = (f32[133]{0:T(256)S(1)}, f32[133]{0:T(256)}, u32[]{:S(2)}) copy-start(f32[133]{0:T(256)} %slice_multiply_fusion.9) | copy-start | bytes 1600

commit v2 on v0

v2 whole, which is shorter than its diff:
```python
import functools

import jax
import jax.numpy as jnp
from jax import lax
from jax.experimental import pallas as pl
from jax.experimental.pallas import tpu as pltpu
from jax.sharding import PartitionSpec as P

STEPS = 2
LANES = 128
MESH = pl.DeviceIdType.MESH

coupling = 0.25


def minmod(first_term, second_term):
    low = jnp.minimum(first_term, second_term)
    high = jnp.maximum(first_term, second_term)
    return jnp.maximum(low, 0.0) + jnp.minimum(high, 0.0)


def step_pair(spectra, open_faces, speeds):
    width = spectra.shape[1]
    forward = jnp.maximum(speeds, 0.0)
    backward = jnp.minimum(speeds, 0.0)
    forward_half = 0.5 * (1.0 - forward)
    backward_half = 0.5 * (1.0 + backward)
    for _ in range(2):
        ahead = pltpu.roll(spectra, width - 1, 1) - spectra
        slopes = minmod(ahead, pltpu.roll(ahead, 1, 1))
        from_left = forward * (spectra + forward_half * slopes)
        from_right = backward * (spectra - backward_half * slopes)
        fluxes = (from_left + pltpu.roll(from_right, width - 1, 1)) * open_faces
        spectra = spectra - (fluxes - pltpu.roll(fluxes, 1, 1))
    return spectra


def kernel(
    n, u_ref, speed_ref, sea_ref, lift_hbm, back_hbm, out_ref,
    sent, got, state, rounded, squared, result, sea, lift, back,
    load_sem, own_sem, send_one, recv_one, send_two, recv_two,
):
    me = lax.axis_index("cell")
    depth = u_ref.shape[0]
    packs = depth // 8
    modes, comps = lift.shape

    barrier = pltpu.get_barrier_semaphore()

    def greet(k, _):
        other = lax.rem(me + k, n)
        pl.semaphore_signal(barrier, inc=1, device_id={"cell": other}, device_id_type=MESH)
        return 0

    lax.fori_loop(1, n, greet, 0)
    load_lift = pltpu.make_async_copy(lift_hbm, lift, load_sem.at[0])
    load_back = pltpu.make_async_copy(back_hbm, back, load_sem.at[1])
    load_lift.start()
    load_back.start()

    cells = n * LANES
    sea_row = sea_ref[...].astype(jnp.float32)
    sea[:, :cells] = jnp.broadcast_to(sea_row, (8, cells))
    sea[:, cells:] = jnp.zeros((8, LANES), jnp.float32)
    all_sea = sea[...]
    all_open = all_sea * pltpu.roll(all_sea, cells + LANES - 1, 1)
    lane = lax.broadcasted_iota(jnp.int32, (8, LANES), 1)

    for g in range(packs):
        rows = pl.ds(g * 8, 8)
        own_rows = pl.ds(pl.multiple_of(me * depth + g * 8, 8), 8)
        block = jnp.concatenate([u_ref[rows, :], jnp.zeros((8, LANES), jnp.float32)], axis=1)
        block = step_pair(block, all_open, speed_ref[own_rows, :])
        tiles = [block[:, t * LANES : (t + 1) * LANES] for t in range(n + 1)]
        for t in range(n):
            sent[t, rows, :] = tiles[t]
            edge = jnp.where(lane < 64, tiles[t + 1], tiles[t - 1])
            if g:
                edge = pltpu.roll(edge, 8 * g, 1)
                mine = (lane >= 8 * g - 4) & (lane < 8 * g + 4)
                edge = jnp.where(mine, edge, sent[t, depth : depth + 8, :])
            sent[t, depth : depth + 8, :] = edge

    def first(dest, source):
        return pltpu.make_async_remote_copy(
            src_ref=sent.at[dest], dst_ref=got.at[source],
            send_sem=send_one.at[dest], recv_sem=recv_one.at[source],
            device_id={"cell": dest}, device_id_type=MESH,
        )

    pl.semaphore_wait(barrier, n - 1)

    def push(k, _):
        first(lax.rem(me + k, n), me).start()
        return 0

    lax.fori_loop(1, n, push, 0)

    main_sea = sea[:, pl.ds(pl.multiple_of(me * LANES, LANES), LANES)]
    next_sea = sea[:, pl.ds(pl.multiple_of((me + 1) * LANES, LANES), LANES)]
    last_tile = lax.rem(me + n, n + 1)
    last_sea = sea[:, pl.ds(pl.multiple_of(last_tile * LANES, LANES), LANES)]
    side_sea = jnp.where(lane < 4, next_sea, jnp.where(lane >= LANES - 4, last_sea, 0.0))
    near_sea = jnp.concatenate([main_sea, side_sea], axis=1)
    near_open = (near_sea * pltpu.roll(near_sea, 2 * LANES - 1, 1))[0:1, :]

    def unpack(source, block):
        halo = (lane < 4) | (lane >= LANES - 4)
        edge = block[depth : depth + 8, :]
        for g in range(packs):
            rows = pl.ds(pl.multiple_of(source * depth + g * 8, 8), 8)
            state[rows, 0:LANES] = block[g * 8 : g * 8 + 8, :]
            turned = pltpu.roll(edge, LANES - 8 * g, 1) if g else edge
            state[rows, LANES:] = jnp.where(halo, turned, 0.0)

    unpack(me, sent[me])

    def pull(k, _):
        source = lax.rem(me + n - k, n)
        first(source, source).wait_recv()
        unpack(source, got[source])
        return 0

    lax.fori_loop(1, n, pull, 0)

    wide = 64

    def narrow(i, _):
        rows = pl.ds(pl.multiple_of(i * wide, wide), wide)
        rounded[rows, :] = state[rows, :].astype(jnp.bfloat16)
        return 0

    lax.fori_loop(0, comps // wide, narrow, 0)

    mode_part, comp_part = modes // 4, comps // 4

    def lifting(width):
        def body(i, _):
            rows = pl.ds(pl.multiple_of(i * mode_part, mode_part), mode_part)
            lifted = jnp.dot(
                lift[rows, :], rounded[:, :width], preferred_element_type=jnp.float32
            )
            squared[rows, :width] = (lifted * lifted).astype(jnp.bfloat16)
            return 0

        lax.fori_loop(0, 4, body, 0)

    load_lift.wait()
    lifting(2 * LANES)
    load_back.wait()

    def source_one(i, _):
        rows = pl.ds(pl.multiple_of(i * comp_part, comp_part), comp_part)
        source = jnp.dot(back[rows, :], squared[...], preferred_element_type=jnp.float32)
        state[rows, :] = state[rows, :] + coupling * source
        return 0

    lax.fori_loop(0, 4, source_one, 0)

    def propagate(i, _):
        rows = pl.ds(pl.multiple_of(i * wide, wide), wide)
        block = step_pair(state[rows, :], near_open, speed_ref[rows, :])[:, :LANES]
        state[rows, 0:LANES] = block
        rounded[rows, 0:LANES] = block.astype(jnp.bfloat16)
        return 0

    lax.fori_loop(0, comps // wide, propagate, 0)
    lifting(LANES)

    def place(source):
        return out_ref.at[:, pl.ds(pl.multiple_of(source * LANES, LANES), LANES)]

    def second(dest, source):
        return pltpu.make_async_remote_copy(
            src_ref=result.at[dest], dst_ref=place(source),
            send_sem=send_two.at[dest], recv_sem=recv_two.at[source],
            device_id={"cell": dest}, device_id_type=MESH,
        )

    own = pltpu.make_async_copy(result.at[me], place(me), own_sem)
    part = n // 4

    def source_two(i, _):
        rows = pl.ds(pl.multiple_of(i * comp_part, comp_part), comp_part)
        source = jnp.dot(
            back[rows, :], squared[:, :LANES], preferred_element_type=jnp.float32
        )
        total = state[rows, 0:LANES] + coupling * source
        result[pl.ds(i * part, part)] = total.reshape(part, depth, LANES)

        def send(j, _):
            dest = i * part + j

            @pl.when(dest != me)
            def _():
                second(dest, me).start()

            return 0

        lax.fori_loop(0, part, send, 0)
        return 0

    lax.fori_loop(0, 4, source_two, 0)
    own.start()

    def finish(k, _):
        dest = lax.rem(me + k, n)
        source = lax.rem(me + n - k, n)
        first(dest, me).wait_send()
        second(dest, me).wait_send()
        second(source, source).wait_recv()
        return 0

    lax.fori_loop(1, n, finish, 0)
    own.wait()


def shards(wave_energy, courant, sea_mask, lift_weight, back_weight):
    n = lax.axis_size("cell")
    groups, cells = wave_energy.shape
    modes = lift_weight.shape[0]
    depth = -(-groups // 8) * 8
    extra = depth - groups
    if extra:
        wave_energy = jnp.pad(wave_energy, ((0, extra), (0, 0)))
        courant = jnp.pad(courant.reshape(n, groups), ((0, 0), (0, extra))).reshape(-1)
        lift_weight = jnp.pad(
            lift_weight.reshape(modes, n, groups), ((0, 0), (0, 0), (0, extra))
        ).reshape(modes, n * depth)
        back_weight = jnp.pad(
            back_weight.reshape(n, groups, modes), ((0, 0), (0, extra), (0, 0))
        ).reshape(n * depth, modes)
    comps = n * depth
    vmem = pl.BlockSpec(memory_space=pltpu.VMEM)
    anywhere = pl.BlockSpec(memory_space=pl.ANY)
    out = pl.pallas_call(
        functools.partial(kernel, n),
        out_shape=jax.ShapeDtypeStruct((depth, cells), jnp.float32),
        in_specs=[vmem, vmem, vmem, anywhere, anywhere],
        out_specs=anywhere,
        scratch_shapes=[
            pltpu.VMEM((n, depth + 8, LANES), jnp.float32),
            pltpu.VMEM((n, depth + 8, LANES), jnp.float32),
            pltpu.VMEM((comps, 2 * LANES), jnp.float32),
            pltpu.VMEM((comps, 2 * LANES), jnp.bfloat16),
            pltpu.VMEM((modes, 2 * LANES), jnp.bfloat16),
            pltpu.VMEM((n, depth, LANES), jnp.float32),
            pltpu.VMEM((8, cells + LANES), jnp.float32),
            pltpu.VMEM((modes, comps), jnp.bfloat16),
            pltpu.VMEM((comps, modes), jnp.bfloat16),
            pltpu.SemaphoreType.DMA((2,)),
            pltpu.SemaphoreType.DMA,
            pltpu.SemaphoreType.DMA((n,)),
            pltpu.SemaphoreType.DMA((n,)),
            pltpu.SemaphoreType.DMA((n,)),
            pltpu.SemaphoreType.DMA((n,)),
        ],
        compiler_params=pltpu.CompilerParams(collective_id=0, has_side_effects=True),
    )(wave_energy, courant[:, None], sea_mask[None, :], lift_weight, back_weight)
    return out[:groups]


def solution(mesh):
    placed = (P(("member", "cell"), None), P(), P(), P(), P())
    return jax.shard_map(
        shards, mesh=mesh, in_specs=placed, out_specs=P(("member", "cell"), None), check_vma=False
    )
```

time: 94.3 us -> 57.9 us (0.61)
  the two profiles are of different devices: /device:TPU:0 before, /device:TPU:31 now
where the time goes in v2:
time: 57.9 us; the launch traced here: 57.7 us
  Pallas kernels  54 us (93%)
  local copies, waits for them, and re-layouts  3.65 us (6%)
    pallas_call x1, Pallas kernels, shards(): pl.pallas_call(functools.partial(kernel, n), out_shape=jax.ShapeDtypeStru...  54 us
    unnamed x1, local copies, waits for them, and re-layouts  1.92 us
    broadcast_in_dim x1, local copies, waits for them, and re-layouts, shards(): courant[:, None]  1.73 us

profile of v2, /device:TPU:31, one launch (start us, length us, event | category | flops | bytes accessed | tf_op | source)
XLA Modules:
  0.0 57.7 jit_solution(8829841044671448064)
XLA Ops:
  0.0 1.7 %broadcast_in_dim.8.speed_ref = f32[1152,1]{1,0:T(8,128)} reshape(f32[1152]{0:T(1024)} %param.6) | data formatting | bytes 9216 | tf_op jit(solution)/shard_map/broadcast_in_dim | solution.py:260
  1.7 54.0 %shard_map.55 = f32[72,2048]{1,0:T(8,128)} custom-call(f32[72,2048]{1,0:T(8,128)} %u_ref.1, f32[1152,1]{1,0:T(8,128)} %broadcast_in_dim.8.speed_ref, s32[1,2048]{1,0:T(1,128)} %bitcast.1, bf16[1024,1152]{1,0:T(8,128)(2,1)} %lift_hbm.1, bf16[1152,1024]{1,0:T(8,128)(2,1)} %back_hbm.1), custom_call_target="tpu_custom_call" | custom-call | tf_op jit(solution)/shard_map/pallas_call | solution.py:237
  55.8 1.9 %copy.8 = f32[72,2048]{1,0:T(8,128)} copy(f32[72,2048]{1,0:T(8,128)} %shard_map.55) | data formatting | bytes 1179648

commit v3 on v2

--- a/solution.py
+++ b/solution.py
@@ -22,23 +22,22 @@
 
 def step_pair(spectra, open_faces, speeds):
     width = spectra.shape[1]
-    forward = jnp.maximum(speeds, 0.0)
-    backward = jnp.minimum(speeds, 0.0)
-    forward_half = 0.5 * (1.0 - forward)
-    backward_half = 0.5 * (1.0 + backward)
+    eastward = speeds >= 0.0
+    weight = jnp.where(eastward, 0.5 * (1.0 - speeds), -0.5 * (1.0 + speeds))
+    open_before = pltpu.roll(open_faces, 1, 1)
     for _ in range(2):
         ahead = pltpu.roll(spectra, width - 1, 1) - spectra
-        slopes = minmod(ahead, pltpu.roll(ahead, 1, 1))
-        from_left = forward * (spectra + forward_half * slopes)
-        from_right = backward * (spectra - backward_half * slopes)
-        fluxes = (from_left + pltpu.roll(from_right, width - 1, 1)) * open_faces
-        spectra = spectra - (fluxes - pltpu.roll(fluxes, 1, 1))
+        behind = spectra - pltpu.roll(spectra, 1, 1)
+        carried = speeds * (spectra + weight * minmod(ahead, behind))
+        after = jnp.where(eastward, carried, pltpu.roll(carried, width - 1, 1))
+        before = jnp.where(eastward, pltpu.roll(carried, 1, 1), carried)
+        spectra = spectra - (after * open_faces - before * open_before)
     return spectra
 
 
 def kernel(
     n, u_ref, speed_ref, sea_ref, lift_hbm, back_hbm, out_ref,
-    sent, got, state, rounded, squared, result, sea, lift, back,
+    sent, got, state, rounded, squared, result, sea, speeds, lift, back,
     load_sem, own_sem, send_one, recv_one, send_two, recv_two,
 ):
     me = lax.axis_index("cell")
@@ -67,11 +66,16 @@
     all_open = all_sea * pltpu.roll(all_sea, cells + LANES - 1, 1)
     lane = lax.broadcasted_iota(jnp.int32, (8, LANES), 1)
 
+    for r in range(speed_ref.shape[0]):
+        row = jnp.broadcast_to(speed_ref[r : r + 1, :], (LANES, LANES))
+        speeds[r * LANES : (r + 1) * LANES, :] = jnp.transpose(row)
+
     for g in range(packs):
         rows = pl.ds(g * 8, 8)
         own_rows = pl.ds(pl.multiple_of(me * depth + g * 8, 8), 8)
         block = jnp.concatenate([u_ref[rows, :], jnp.zeros((8, LANES), jnp.float32)], axis=1)
-        block = step_pair(block, all_open, speed_ref[own_rows, :])
+        own_speeds = jnp.concatenate([speeds[own_rows, :]] * (n + 1), axis=1)
+        block = step_pair(block, all_open, own_speeds)
         tiles = [block[:, t * LANES : (t + 1) * LANES] for t in range(n + 1)]
         for t in range(n):
             sent[t, rows, :] = tiles[t]
@@ -158,18 +162,28 @@
 
     lax.fori_loop(0, 4, source_one, 0)
 
+    slab, piece = 128, 32
+    near_open = jnp.broadcast_to(near_open, (piece, 2 * LANES))
+
     def propagate(i, _):
-        rows = pl.ds(pl.multiple_of(i * wide, wide), wide)
-        block = step_pair(state[rows, :], near_open, speed_ref[rows, :])[:, :LANES]
-        state[rows, 0:LANES] = block
-        rounded[rows, 0:LANES] = block.astype(jnp.bfloat16)
-        return 0
-
-    lax.fori_loop(0, comps // wide, propagate, 0)
+        spans = [
+            pl.ds(pl.multiple_of(i * slab + j * piece, piece), piece) for j in range(slab // piece)
+        ]
+        before = [state[rows, :] for rows in spans]
+        after = [
+            step_pair(block, near_open, jnp.concatenate([speeds[rows, :]] * 2, axis=1))
+            for rows, block in zip(spans, before)
+        ]
+        for rows, block in zip(spans, after):
+            state[rows, 0:LANES] = block[:, :LANES]
+            rounded[rows, 0:LANES] = block[:, :LANES].astype(jnp.bfloat16)
+        return 0
+
+    lax.fori_loop(0, comps // slab, propagate, 0)
     lifting(LANES)
 
     def place(source):
-        return out_ref.at[:, pl.ds(pl.multiple_of(source * LANES, LANES), LANES)]
+        return out_ref.at[source]
 
     def second(dest, source):
         return pltpu.make_async_remote_copy(
@@ -232,11 +246,12 @@
             back_weight.reshape(n, groups, modes), ((0, 0), (0, extra), (0, 0))
         ).reshape(n * depth, modes)
     comps = n * depth
+    speed_rows = jnp.pad(courant, (0, -comps % LANES)).reshape(-1, LANES)
     vmem = pl.BlockSpec(memory_space=pltpu.VMEM)
     anywhere = pl.BlockSpec(memory_space=pl.ANY)
     out = pl.pallas_call(
         functools.partial(kernel, n),
-        out_shape=jax.ShapeDtypeStruct((depth, cells), jnp.float32),
+        out_shape=jax.ShapeDtypeStruct((n, depth, cells // n), jnp.float32),
         in_specs=[vmem, vmem, vmem, anywhere, anywhere],
         out_specs=anywhere,
         scratch_shapes=[
@@ -247,6 +262,7 @@
             pltpu.VMEM((modes, 2 * LANES), jnp.bfloat16),
             pltpu.VMEM((n, depth, LANES), jnp.float32),
             pltpu.VMEM((8, cells + LANES), jnp.float32),
+            pltpu.VMEM((speed_rows.size, LANES), jnp.float32),
             pltpu.VMEM((modes, comps), jnp.bfloat16),
             pltpu.VMEM((comps, modes), jnp.bfloat16),
             pltpu.SemaphoreType.DMA((2,)),
@@ -257,8 +273,8 @@
             pltpu.SemaphoreType.DMA((n,)),
         ],
         compiler_params=pltpu.CompilerParams(collective_id=0, has_side_effects=True),
-    )(wave_energy, courant[:, None], sea_mask[None, :], lift_weight, back_weight)
-    return out[:groups]
+    )(wave_energy, speed_rows, sea_mask[None, :], lift_weight, back_weight)
+    return out.transpose(1, 0, 2).reshape(depth, cells)[:groups]
 
 
 def solution(mesh):

time: 57.9 us -> 48.6 us (0.84)
  Pallas kernels: 54 us -> 46.5 us
  local copies, waits for them, and re-layouts: 3.65 us -> 1.93 us
    pallas_call x1, Pallas kernels: 54 us -> 46.5 us  [shards(): pl.pallas_call(functools.partial(kernel, n), out_shape=jax.ShapeDtypeStru...]
    reshape x0 -> x1, local copies, waits for them, and re-layouts: none -> 1.93 us  [shards(): return out.transpose(1, 0, 2).reshape(depth, cells)[:groups]]
    unnamed x1 -> x0, local copies, waits for them, and re-layouts: 1.92 us -> none
    broadcast_in_dim x1 -> x0, local copies, waits for them, and re-layouts: 1.73 us -> none  [shards(): courant[:, None]]
where the time goes in v3:
time: 48.6 us; the launch traced here: 48.5 us
  Pallas kernels  46.5 us (96%)
  local copies, waits for them, and re-layouts  1.93 us (4%)
    pallas_call x1, Pallas kernels, shards(): pl.pallas_call(functools.partial(kernel, n), out_shape=jax.ShapeDtypeStru...  46.5 us
    reshape x1, local copies, waits for them, and re-layouts, shards(): return out.transpose(1, 0, 2).reshape(depth, cells)[:groups]  1.93 us

profile of v3, /device:TPU:31, one launch (start us, length us, event | category | flops | bytes accessed | tf_op | source)
XLA Modules:
  0.0 48.5 jit_solution(16218325384811514759)
XLA Ops:
  0.0 46.5 %shard_map.55 = f32[16,72,128]{2,1,0:T(8,128)} custom-call(f32[72,2048]{1,0:T(8,128)} %u_ref.1, f32[9,128]{1,0:T(8,128)} %bitcast.8, s32[1,2048]{1,0:T(1,128)} %bitcast.9, bf16[1024,1152]{1,0:T(8,128)(2,1)} %lift_hbm.1, bf16[1152,1024]{1,0:T(8,128)(2,1)} %back_hbm.1), custom_call_target="tpu_custom_call" | custom-call | tf_op jit(solution)/shard_map/pallas_call | solution.py:252
  46.5 1.9 %copy_bitcast_fusion = f32[72,2048]{1,0:T(8,128)} fusion(f32[16,72,128]{2,1,0:T(8,128)} %shard_map.55), kind=kLoop, calls=%fused_computation | loop fusion | bytes 1179648 | tf_op jit(solution)/shard_map/reshape | solution.py:277

commit v4 on v3

--- a/solution.py
+++ b/solution.py
@@ -96,7 +96,7 @@
     pl.semaphore_wait(barrier, n - 1)
 
     def push(k, _):
-        first(lax.rem(me + k, n), me).start()
+        first(lax.rem(me + n - k, n), me).start()
         return 0
 
     lax.fori_loop(1, n, push, 0)
@@ -121,7 +121,7 @@
     unpack(me, sent[me])
 
     def pull(k, _):
-        source = lax.rem(me + n - k, n)
+        source = lax.rem(me + k, n)
         first(source, source).wait_recv()
         unpack(source, got[source])
         return 0
@@ -195,7 +195,8 @@
     own = pltpu.make_async_copy(result.at[me], place(me), own_sem)
     part = n // 4
 
-    def source_two(i, _):
+    def source_two(step, _):
+        i = lax.rem(me // part + 1 + step, 4)
         rows = pl.ds(pl.multiple_of(i * comp_part, comp_part), comp_part)
         source = jnp.dot(
             back[rows, :], squared[:, :LANES], preferred_element_type=jnp.float32

time: 48.6 us -> 46.4 us (0.955)
  the two profiles are of different devices: /device:TPU:31 before, /device:TPU:0 now
where the time goes in v4:
time: 46.4 us; the launch traced here: 46.2 us
  Pallas kernels  44.3 us (95%)
  local copies, waits for them, and re-layouts  1.93 us (4%)
    pallas_call x1, Pallas kernels, shards(): pl.pallas_call(functools.partial(kernel, n), out_shape=jax.ShapeDtypeStru...  44.3 us
    reshape x1, local copies, waits for them, and re-layouts, shards(): return out.transpose(1, 0, 2).reshape(depth, cells)[:groups]  1.93 us

profile of v4, /device:TPU:0, one launch (start us, length us, event | category | flops | bytes accessed | tf_op | source)
XLA Modules:
  0.0 46.2 jit_solution(2003654355907894468)
XLA Ops:
  0.0 44.3 %shard_map.55 = f32[16,72,128]{2,1,0:T(8,128)} custom-call(f32[72,2048]{1,0:T(8,128)} %u_ref.1, f32[9,128]{1,0:T(8,128)} %bitcast.8, s32[1,2048]{1,0:T(1,128)} %bitcast.9, bf16[1024,1152]{1,0:T(8,128)(2,1)} %lift_hbm.1, bf16[1152,1024]{1,0:T(8,128)(2,1)} %back_hbm.1), custom_call_target="tpu_custom_call" | custom-call | tf_op jit(solution)/shard_map/pallas_call | solution.py:253
  44.3 1.9 %copy_bitcast_fusion = f32[72,2048]{1,0:T(8,128)} fusion(f32[16,72,128]{2,1,0:T(8,128)} %shard_map.55), kind=kLoop, calls=%fused_computation | loop fusion | bytes 1179648 | tf_op jit(solution)/shard_map/reshape | solution.py:278

commit v5 on v4

--- a/solution.py
+++ b/solution.py
@@ -137,7 +137,7 @@
 
     lax.fori_loop(0, comps // wide, narrow, 0)
 
-    mode_part, comp_part = modes // 4, comps // 4
+    mode_part, comp_part = modes // 2, comps // 4
 
     def lifting(width):
         def body(i, _):
@@ -148,7 +148,7 @@
             squared[rows, :width] = (lifted * lifted).astype(jnp.bfloat16)
             return 0
 
-        lax.fori_loop(0, 4, body, 0)
+        lax.fori_loop(0, 2, body, 0)
 
     load_lift.wait()
     lifting(2 * LANES)

time: 46.4 us -> 45.8 us (0.987)
  Pallas kernels: 44.3 us -> 43.7 us
    pallas_call x1, Pallas kernels: 44.3 us -> 43.7 us  [shards(): pl.pallas_call(functools.partial(kernel, n), out_shape=jax.ShapeDtypeStru...]
where the time goes in v5:
time: 45.8 us; the launch traced here: 45.6 us
  Pallas kernels  43.7 us (95%)
  local copies, waits for them, and re-layouts  1.93 us (4%)
    pallas_call x1, Pallas kernels, shards(): pl.pallas_call(functools.partial(kernel, n), out_shape=jax.ShapeDtypeStru...  43.7 us
    reshape x1, local copies, waits for them, and re-layouts, shards(): return out.transpose(1, 0, 2).reshape(depth, cells)[:groups]  1.93 us

profile of v5, /device:TPU:0, one launch (start us, length us, event | category | flops | bytes accessed | tf_op | source)
XLA Modules:
  0.0 45.6 jit_solution(11717158003484497679)
XLA Ops:
  0.0 43.7 %shard_map.55 = f32[16,72,128]{2,1,0:T(8,128)} custom-call(f32[72,2048]{1,0:T(8,128)} %u_ref.1, f32[9,128]{1,0:T(8,128)} %bitcast.8, s32[1,2048]{1,0:T(1,128)} %bitcast.9, bf16[1024,1152]{1,0:T(8,128)(2,1)} %lift_hbm.1, bf16[1152,1024]{1,0:T(8,128)(2,1)} %back_hbm.1), custom_call_target="tpu_custom_call" | custom-call | tf_op jit(solution)/shard_map/pallas_call | solution.py:253
  43.7 1.9 %copy_bitcast_fusion = f32[72,2048]{1,0:T(8,128)} fusion(f32[16,72,128]{2,1,0:T(8,128)} %shard_map.55), kind=kLoop, calls=%fused_computation | loop fusion | bytes 1179648 | tf_op jit(solution)/shard_map/reshape | solution.py:278
